TPU v7x, 128 devices: a whole 4x4x4 slice. The times are simulated.
128 devices in a mesh: tile: 16 (over y, z), depth: 8 (over x, core).
Axes of the slice: x: 4, y: 4, z: 4, core: 2. Of those that a mesh axis runs over, the one named last changes fastest.
Arguments:
- owned_blocks: bfloat16 [8, 1024, 32768], P('depth', 'tile'), may hold values from -6 to 6
- slot_counts: int32 [8, 16], P('depth'), may hold values from 1 to 64, 512 in all within a row
- brick_order: int32 [8, 16], P('depth'), may hold values from 0 to 15, each once within a row
- view_flip: int32 [16], replicated, may hold values from 0 to 1
- tf_centers: float32 [8], replicated, may hold values from -2.5 to 2.5
- tf_amps: float32 [4, 8], replicated, may hold values from -6 to 6
Outputs:
- image: float32 [4, 128, 2048], P(None, 'depth', 'tile')
Inputs may be any that keep to these rules, and one draw needn't show every extreme that they name: `slot_counts`: every row sums to 512, and some entry of every row equals 64. `brick_order`: every row holds each of 0 to 15 once.
All inputs are finite; a program needn't handle non-finite values.
Results may differ from a plain program's by a relative error of at most 0.0003.
Values may be sent and summed in bfloat16 or wider, within the bound.
A program may use at most 64 MiB of HBM per device.

v0:
```python
import jax
import jax.numpy as jnp
from jax import lax
from jax.sharding import PartitionSpec as P

BLOCK = 32
BX = 4
BY = 4
DB = 2
KNOTS = 8


bump_scale = 4.0


def swapped(block, axis, bit):
    count = lax.axis_size(axis)
    route = []
    for low in range(count):
        high = low | 1 << bit
        if high != low and high < count:
            route += [(low, high), (high, low)]
    return lax.ppermute(block, axis, route)


def select_entry(table, index, tile_lane):
    return jnp.sum(jnp.where(tile_lane == index, table, 0))


def over_blend(nearer, farther, chan_axis):
    coverage = lax.slice_in_dim(nearer, 3, 4, axis=chan_axis)
    return nearer + (1.0 - coverage) * farther


def march_blocks(blocks, flip_rows, tf_centers, tf_amps, step_size):
    block_count = blocks.shape[0]
    values = blocks.reshape(block_count, BLOCK, BLOCK * BLOCK).astype(jnp.float32)
    fields = [jnp.zeros_like(values) for channel in range(4)]
    for knot_index in range(KNOTS):
        bump_term = jnp.exp(-bump_scale * jnp.square(values - tf_centers[knot_index]))
        fields = [
            fields[channel] + tf_amps[channel, knot_index] * bump_term for channel in range(4)
        ]
    extinction = jax.nn.softplus(fields[3])
    opacity_step = 1.0 - jnp.exp(-step_size * extinction)
    depth_row = lax.broadcasted_iota(jnp.int32, (BLOCK, BLOCK), 0)
    depth_col = lax.broadcasted_iota(jnp.int32, (BLOCK, BLOCK), 1)
    lower_mask = (depth_col < depth_row).astype(jnp.float32)
    upper_mask = (depth_col > depth_row).astype(jnp.float32)
    weights = jnp.where(flip_rows[:, None, None] == 1, upper_mask[None], lower_mask[None])
    before = jnp.einsum("nzw,nwp->nzp", weights, extinction, precision=lax.Precision.HIGHEST)
    passed = jnp.exp(-step_size * before) * opacity_step
    colors = [jnp.sum(passed * jax.nn.sigmoid(fields[channel]), axis=1) for channel in range(3)]
    opacity = 1.0 - jnp.exp(-step_size * jnp.sum(extinction, axis=1))
    return jnp.stack(colors + [opacity], axis=1)


def body(owned_blocks, slot_counts, brick_order, view_flip, tf_centers, tf_amps):
    tile_count = lax.axis_size("tile")
    depth_count = lax.axis_size("depth")
    mine_tile = lax.axis_index("tile")
    depth_index = lax.axis_index("depth")
    step_size = 1.5 / (depth_count * DB * BLOCK)
    tile_lane = jnp.arange(tile_count, dtype=jnp.int32)
    counts = slot_counts[0]
    order_row = brick_order[0]
    starts = jnp.cumsum(counts) - counts
    start_mine = select_entry(starts, mine_tile, tile_lane)
    position = jnp.sum(
        jnp.where(order_row[None, :] == tile_lane[:, None], tile_lane[None, :], 0), axis=1
    )
    position_mine = select_entry(position, mine_tile, tile_lane)
    flip_mine = select_entry(view_flip, mine_tile, tile_lane)
    slot_total = owned_blocks.shape[1]
    capacity = slot_total // tile_count
    brick_total = slot_total // 2
    offsets = jnp.mod(position - start_mine, tile_count)
    send_slots = (
        offsets[:, None] + tile_count * jnp.arange(capacity, dtype=jnp.int32)[None, :]
    ).reshape(-1)
    wanted = jnp.arange(brick_total, dtype=jnp.int32) * tile_count + position_mine
    owner_index = jnp.sum((starts[None, :] <= wanted[:, None]).astype(jnp.int32), axis=1) - 1
    owner_start = jnp.sum(
        jnp.where(tile_lane[None, :] == owner_index[:, None], starts[None, :], 0), axis=1
    )
    row_index = owner_index * capacity + (wanted - owner_start) // tile_count
    outgoing = jnp.take(owned_blocks[0], send_slots, axis=0)
    arrived = lax.all_to_all(outgoing, "tile", split_axis=0, concat_axis=0, tiled=True)
    brick_blocks = jnp.take(arrived, row_index, axis=0)
    flip_rows = jnp.zeros((brick_total,), jnp.int32) + flip_mine
    partial_value = march_blocks(brick_blocks, flip_rows, tf_centers, tf_amps, step_size)
    layers = partial_value.reshape(DB, BY, BX, 4, BLOCK * BLOCK)
    nearest_first = jnp.where(flip_mine == 1, layers[::-1], layers)
    combined = nearest_first[DB - 1]
    combined = over_blend(nearest_first[0], combined, 2)
    tile_image = (
        combined.reshape(BY, BX, 4, BLOCK, BLOCK)
        .transpose(2, 0, 3, 1, 4)
        .reshape(4, BY * BLOCK, BX * BLOCK)
    )
    levels = depth_count.bit_length() - 1
    row_share = tile_image.shape[1] // depth_count
    width = tile_image.shape[2]
    current = tile_image.reshape((4,) + (2,) * levels + (row_share, width))
    for bit_index in range(levels):
        split_axis = 1 + (levels - 1 - bit_index)
        lower_half = lax.slice_in_dim(current, 0, 1, axis=split_axis)
        upper_half = lax.slice_in_dim(current, 1, 2, axis=split_axis)
        high_side = depth_index >> bit_index & 1
        kept_half = jnp.where(high_side == 1, upper_half, lower_half)
        given_half = jnp.where(high_side == 1, lower_half, upper_half)
        other_half = swapped(given_half, "depth", bit_index)
        mine_front = high_side == flip_mine
        current = jnp.where(
            mine_front, over_blend(kept_half, other_half, 0), over_blend(other_half, kept_half, 0)
        )
    result = current.reshape(4, row_share, width)
    return result


def solution(mesh):
    in_specs = (P("depth", "tile", None), P("depth", None), P("depth", None), P(), P(), P())
    out_specs = P(None, "depth", "tile")
    return jax.shard_map(body, mesh=mesh, in_specs=in_specs, out_specs=out_specs, check_vma=False)
```

profile of v0, /device:TPU:114, one launch (start us, length us, event | category | flops | bytes accessed | tf_op | source)
XLA Modules:
  0.0 223.4 jit_solution(15224825677911472230)
XLA Ops:
  0.0 0.8 select_reduce_fusion.1
  0.8 0.7 copy.11
  1.5 0.1 reduce
  1.7 1.3 fusion.115
  3.0 1.2 select_reduce_fusion.2
  4.2 0.1 broadcast_add_fusion
  4.3 0.1 compare_and_fusion
  4.4 0.1 add.271
  4.5 11.4 %gather_fusion = bf16[64,32768]{1,0:T(8,128)(2,1)} fusion(bf16[64,32768]{1,0:T(8,128)(2,1)} %bitcast.98, s32[1024]{0:T(1024)S(1)} %pad_clamp_fusion.1), kind=kCustom, calls=%fused_computation | custom fusion | bytes 8388864 | tf_op jit(solution)/shard_map/jit(_take)/gather | solution.py:87
  15.9 7.2 %gather.13 = bf16[16,4,32768]{2,1,0:T(4,128)(2,1)} reshape(bf16[64,32768]{1,0:T(8,128)(2,1)} %gather_fusion) | data formatting | bytes 8388608 | tf_op jit(solution)/shard_map/jit(_take)/gather | solution.py:87
  23.1 6.0 %broadcast_select_fusion = bf16[16,4,32768]{2,1,0:T(4,128)(2,1)} fusion(bf16[16,4,32768]{2,1,0:T(4,128)(2,1)} %gather.13, pred[16,4]{1,0:T(8,128)(4,1)S(1)} %compare_and_fusion), kind=kLoop, calls=%fused_computation.114 | loop fusion | flops 2097152 | bytes 8388672 | tf_op jit(solution)/shard_map/jit(_take)/select_n | solution.py:87
  29.1 0.0 copy-start.4
  29.1 0.0 copy-start.3
  29.1 0.0 copy-start.2
  29.1 7.1 %all-to-all-start = ((bf16[16,4,32768]{2,1,0:T(4,128)(2,1)}), bf16[16,4,32768]{2,1,0:T(4,128)(2,1)}, u32[]{:S(2)}, u32[]{:S(2)}) async-start(bf16[16,4,32768]{2,1,0:T(4,128)(2,1)} %broadcast_select_fusion), calls=%async_computation | async-start | bytes 8388608 | tf_op jit(solution)/shard_map/all_to_all | solution.py:88
  38.7 0.6 multiply_add_fusion
  39.3 0.0 copy-done.4
  39.3 0.1 convert_reduce_fusion
  39.4 0.1 select_reduce_fusion
  39.5 0.6 fusion.112
  40.1 0.0 copy-done.3
  40.1 0.7 fusion.119
  40.8 0.0 copy-done.2
  40.8 0.7 fusion.118
  41.5 0.7 fusion.117
  42.2 0.6 compare_and_fusion.1
  42.8 59.6 %all-to-all-done = bf16[16,4,32768]{2,1,0:T(4,128)(2,1)} async-done(((bf16[16,4,32768]{2,1,0:T(4,128)(2,1)}), bf16[16,4,32768]{2,1,0:T(4,128)(2,1)}, u32[]{:S(2)}, u32[]{:S(2)}) %all-to-all-start) | async-done | bytes 4194336 | tf_op jit(solution)/shard_map/all_to_all | solution.py:88
  102.4 7.0 %all_to_all.7 = bf16[64,32768]{1,0:T(8,128)(2,1)} reshape(bf16[16,4,32768]{2,1,0:T(4,128)(2,1)} %all-to-all-done) | data formatting | bytes 8388608 | tf_op jit(solution)/shard_map/all_to_all | solution.py:88
  109.4 6.4 %gather_fusion.1 = bf16[32,32768]{1,0:T(8,128)(2,1)S(1)} fusion(bf16[64,32768]{1,0:T(8,128)(2,1)} %all_to_all.7, s32[1024]{0:T(1024)S(1)} %pad_clamp_fusion), kind=kCustom, calls=%fused_computation.1 | custom fusion | bytes 4194432 | tf_op jit(solution)/shard_map/jit(_take)/gather | solution.py:89
  115.8 1.2 copy.13
  117.0 0.0 copy-start
  117.0 21.6 %fusion.116 = (f32[32,1024]{1,0:T(8,128)S(1)}, f32[32,32,1024]{2,1,0:T(8,128)}) fusion(f32[]{:T(128)} %bitcast.24, f32[]{:T(128)} %bitcast.23, f32[]{:T(128)} %bitcast.22, f32[]{:T(128)} %bitcast.21, f32[]{:T(128)} %bitcast.20, f32[]{:T(128)} %bitcast.19, f32[]{:T(128)} %bitcast.18, f32[]{:T(128)} %bitcast.17, f32[]{:T(128)} %bitcast.16, f32[]{:T(128)} %bitcast.15, ...), kind=kLoop, calls=%fused_computation.189 | loop fusion | flops 50298880 | bytes 6422624 | tf_op jit(solution)/shard_map/reduce_sum | solution.py:54
  138.6 0.0 copy-done
  138.6 0.2 sub.162
  138.8 0.0 copy-start.1
  138.8 28.2 %fusion.99 = (f32[32,1024]{1,0:T(8,128)S(1)}, f32[32,32,1024]{2,1,0:T(8,128)}) fusion(f32[]{:T(128)} %bitcast.48, f32[]{:T(128)} %bitcast.47, f32[]{:T(128)} %bitcast.46, f32[]{:T(128)} %bitcast.45, f32[]{:T(128)} %bitcast.44, f32[]{:T(128)} %bitcast.43, f32[]{:T(128)} %bitcast.42, f32[]{:T(128)} %bitcast.41, f32[]{:T(128)} %bitcast.24, f32[]{:T(128)} %bitcast.22, ...), kind=kOutput, calls=%fused_computation.111 | convolution fusion | flops 455049216 | bytes 10621024 | tf_op jit(solution)/shard_map/nzw,nwp->nzp/dot_general | solution.py:51
  167.0 0.2 stack.15
  167.2 0.0 copy-done.1
  167.2 20.2 %fusion.100 = f32[32,1024]{1,0:T(8,128)S(1)} fusion(f32[32,32,1024]{2,1,0:T(8,128)} %get-tuple-element.59, f32[]{:T(128)} %bitcast.40, f32[]{:T(128)} %bitcast.39, f32[]{:T(128)} %bitcast.38, f32[]{:T(128)} %bitcast.37, f32[]{:T(128)} %bitcast.36, f32[]{:T(128)} %bitcast.35, f32[]{:T(128)} %bitcast.34, f32[]{:T(128)} %bitcast.33, f32[]{:T(128)} %bitcast.24, ...), kind=kLoop, calls=%fused_computation.112 | loop fusion | flops 48201728 | bytes 6422624 | tf_op jit(solution)/shard_map/reduce_sum | solution.py:53
  187.4 0.2 stack.14
  187.5 20.3 %fusion.101 = f32[32,1024]{1,0:T(8,128)S(1)} fusion(f32[32,32,1024]{2,1,0:T(8,128)} %get-tuple-element.59, f32[]{:T(128)} %bitcast.32, f32[]{:T(128)} %bitcast.31, f32[]{:T(128)} %bitcast.30, f32[]{:T(128)} %bitcast.29, f32[]{:T(128)} %bitcast.28, f32[]{:T(128)} %bitcast.27, f32[]{:T(128)} %bitcast.26, f32[]{:T(128)} %bitcast.25, f32[]{:T(128)} %bitcast.24, ...), kind=kLoop, calls=%fused_computation.113 | loop fusion | flops 48201728 | bytes 6422624 | tf_op jit(solution)/shard_map/reduce_sum | solution.py:53
  207.9 0.2 stack.13
  208.0 0.5 pad_maximum_fusion
  208.6 0.1 reverse_select_fusion
  208.7 0.1 slice_bitcast_fusion
  208.8 0.4 squeeze.176
  209.2 0.4 squeeze.178
  209.6 0.2 fusion.103
  209.8 0.1 mul.459
  209.9 0.3 add_bitcast_fusion
  210.2 0.7 copy.12
  210.9 0.5 reshape_reshape.3
  211.4 0.1 collective-permute-start
  211.5 1.3 collective-permute-done
  212.9 0.6 collective-permute-start.1
  213.5 3.7 %collective-permute-done.1 = f32[4,2,1,1,16,128]{5,4,3,2,1,0:T(8,128)S(1)} collective-permute-done((f32[4,2,1,1,16,128]{5,4,3,2,1,0:T(8,128)S(1)}, f32[4,2,1,1,16,128]{5,4,3,2,1,0:T(8,128)S(1)}, u32[]{:S(2)}, u32[]{:S(2)}) %collective-permute-start.1) | collective-permute-done | bytes 65568 | tf_op jit(solution)/shard_map/ppermute | solution.py:23
  217.3 2.2 collective-permute-start.2
  219.5 3.3 %collective-permute-done.2 = f32[4,1,1,1,16,128]{5,4,3,2,1,0:T(8,128)S(1)} collective-permute-done((f32[4,1,1,1,16,128]{5,4,3,2,1,0:T(8,128)S(1)}, f32[4,1,1,1,16,128]{5,4,3,2,1,0:T(8,128)S(1)}, u32[]{:S(2)}, u32[]{:S(2)}) %collective-permute-start.2) | collective-permute-done | bytes 32800 | tf_op jit(solution)/shard_map/ppermute | solution.py:23
  222.8 0.6 select_bitcast_fusion
  (20 shorter events, 0.2 us)
Async XLA Ops:
  29.1 10.2 %copy-start.4 = (s32[1,16]{1,0:T(1,128)S(1)}, s32[1,16]{1,0:T(1,128)}, u32[]{:S(2)}) copy-start(s32[1,16]{1,0:T(1,128)} %param.7) | copy-start | bytes 196
  29.1 11.0 %copy-start.3 = (f32[8]{0:T(128)S(1)}, f32[8]{0:T(128)}, u32[]{:S(2)}) copy-start(f32[8]{0:T(128)} %param.10) | copy-start | bytes 100
  29.1 11.7 %copy-start.2 = (f32[4,8]{1,0:T(4,128)S(1)}, f32[4,8]{1,0:T(4,128)}, u32[]{:S(2)}) copy-start(f32[4,8]{1,0:T(4,128)} %param.11) | copy-start | bytes 388
  29.1 73.3 %all-to-all-start = ((bf16[16,4,32768]{2,1,0:T(4,128)(2,1)}), bf16[16,4,32768]{2,1,0:T(4,128)(2,1)}, u32[]{:S(2)}, u32[]{:S(2)}) async-start(bf16[16,4,32768]{2,1,0:T(4,128)(2,1)} %broadcast_select_fusion), calls=%async_computation | async-start | bytes 8388608 | tf_op jit(solution)/shard_map/all_to_all | solution.py:88
  117.0 21.6 %copy-start = (bf16[4,8,32,1024]{3,2,1,0:T(8,128)(2,1)}, bf16[4,8,32,1024]{3,2,1,0:T(8,128)(2,1)S(1)}, u32[]{:S(2)}) copy-start(bf16[4,8,32,1024]{3,2,1,0:T(8,128)(2,1)S(1)} %copy.13) | copy-start | bytes 6291460
  138.8 28.4 %copy-start.1 = (bf16[4,8,32,1024]{3,2,1,0:T(8,128)(2,1)S(1)}, bf16[4,8,32,1024]{3,2,1,0:T(8,128)(2,1)}, u32[]{:S(2)}) copy-start(bf16[4,8,32,1024]{3,2,1,0:T(8,128)(2,1)} %copy-done) | copy-start | bytes 6291460
  211.4 1.4 collective-permute-start
  212.9 4.3 %collective-permute-start.1 = (f32[4,2,1,1,16,128]{5,4,3,2,1,0:T(8,128)S(1)}, f32[4,2,1,1,16,128]{5,4,3,2,1,0:T(8,128)S(1)}, u32[]{:S(2)}, u32[]{:S(2)}) collective-permute-start(f32[4,2,1,1,16,128]{5,4,3,2,1,0:T(8,128)S(1)} %get-tuple-element.13), channel_id=1, source_target_pairs={{0,2},{2,0},{1,3},{3,1},{4,6},{6,4},{5,7},{7,5},{8,10},{10,8},{9,1... | collective-permute-start | bytes 196616 | tf_op jit(solution)/shard_map/ppermute | solution.py:23
  217.3 5.5 %collective-permute-start.2 = (f32[4,1,1,1,16,128]{5,4,3,2,1,0:T(8,128)S(1)}, f32[4,1,1,1,16,128]{5,4,3,2,1,0:T(8,128)S(1)}, u32[]{:S(2)}, u32[]{:S(2)}) collective-permute-start(f32[4,1,1,1,16,128]{5,4,3,2,1,0:T(8,128)S(1)} %get-tuple-element.15), channel_id=1, source_target_pairs={{0,4},{4,0},{1,5},{5,1},{2,6},{6,2},{3,7},{7,3},{8,12},{12,8},{9,1... | collective-permute-start | bytes 98312 | tf_op jit(solution)/shard_map/ppermute | solution.py:23
where the time goes:
time: 225 us; the launch traced here: 223 us
  other arithmetic  75.7 us (34%)
  waiting for transfers between devices  67.9 us (30%)
  local copies, waits for them, and re-layouts  38.8 us (17%)
  matrix products  28.2 us (13%)
  starting transfers between devices  9.96 us (4%)
  between operations  2.81 us (1%)
    all_to_all x1, waiting for transfers between devices, body(): lax.all_to_all(outgoing, 'tile', split_axis=0, concat_axis=0, tiled=True)  59.6 us
    reduce_sum x2, other arithmetic, march_blocks(): jnp.sum(passed * jax.nn.sigmoid(fields[channel]), axis=1)  40.5 us
    dot_general x1, matrix products, march_blocks(): jnp.einsum('nzw,nwp->nzp', weights, extinction, precision=lax.Precision.H...  28.2 us
    reduce_sum x1, other arithmetic, march_blocks(): opacity = 1.0 - jnp.exp(-step_size * jnp.sum(extinction, axis=1))  21.6 us
    gather x2, local copies, waits for them, and re-layouts, body(): outgoing = jnp.take(owned_blocks[0], send_slots, axis=0)  18.6 us
    ppermute x3, waiting for transfers between devices, swapped(): return lax.ppermute(block, axis, route)  8.35 us
    all_to_all x1, starting transfers between devices, body(): lax.all_to_all(outgoing, 'tile', split_axis=0, concat_axis=0, tiled=True)  7.06 us
    all_to_all x1, local copies, waits for them, and re-layouts, body(): lax.all_to_all(outgoing, 'tile', split_axis=0, concat_axis=0, tiled=True)  6.98 us
  transfers between devices with their start and end apart: 4, of which 4 were waited for; matrix products, arithmetic and copies ran while one was open for 2% of the time, Pallas kernels for 0%

commit v1 on v0

v1 whole, which is shorter than its diff:
```python
import functools

import jax
import jax.numpy as jnp
from jax import lax
from jax.experimental import pallas as pl
from jax.experimental.pallas import tpu as pltpu
from jax.sharding import PartitionSpec as P

MESH = pl.DeviceIdType.MESH
BLOCK = 32
KNOTS = 8
N_TILE = 16
N_DEPTH = 8
GROUPS = 4
LANES = 128
PIXELS = BLOCK * BLOCK
CHUNKS = PIXELS // LANES
STEP = 1.5 / 512


def march(vox, img, sign, row0, chunk, centers, amps):
    step_sign = sign * STEP

    def body(z, carry):
        total, held, red, green, blue = carry
        lane = pl.multiple_of(z * PIXELS + chunk * LANES, LANES)
        value = vox[pl.ds(row0, N_TILE), pl.ds(lane, LANES)].astype(jnp.float32)
        fields = [None] * 4
        for k in range(KNOTS):
            off = value - centers[k]
            bump = jnp.exp(off * off * -4.0)
            for c in range(4):
                term = amps[c][k] * bump
                fields[c] = term if k == 0 else fields[c] + term
        total = total + jnp.log(1.0 + jnp.exp(fields[3]))
        now = jnp.exp(total * step_sign)
        weight = held - now
        red = red + weight * jnp.tanh(fields[0])
        green = green + weight * jnp.tanh(fields[1])
        blue = blue + weight * jnp.tanh(fields[2])
        return total, now, red, green, blue

    zero = jnp.zeros((N_TILE, LANES), jnp.float32)
    total, held, red, green, blue = lax.fori_loop(
        0, BLOCK, body, (zero, zero + 1.0, zero, zero, zero), unroll=4
    )
    through = jnp.exp(total * -STEP)
    scale = jnp.where(sign < 0.0, 0.5, -0.5 * through)
    half = chunk // 4
    quarter = chunk % 4
    for c, colour in enumerate((red, green, blue)):
        img[half * 16 + c * 4 + quarter] = scale * ((1.0 - held) + colour)
    img[half * 16 + 12 + quarter] = 1.0 - through


def over(nearer, farther):
    low, high = nearer[0:8], nearer[8:16]
    clear = 1.0 - high
    clear = jnp.concatenate([clear[4:8], clear[4:8]], axis=0)
    return jnp.concatenate([low + clear * farther[0:8], high + clear * farther[8:16]], axis=0)


def render(
    counts, order, flips, centers_ref, amps_ref, blocks, out,
    vox, img, send, recv, dsend, drecv, starts, rows, found,
    load_sem, send_sem, recv_sem, dsend_sem, drecv_sem,
):
    me = lax.axis_index("tile")
    my_depth = lax.axis_index("depth")
    loads = []
    for m in range(GROUPS):
        part = pl.ds(m * N_TILE, N_TILE)
        load = pltpu.make_async_copy(blocks.at[part, :], vox.at[part, :], load_sem.at[m])
        load.start()
        loads.append(load)
    barrier = pltpu.get_barrier_semaphore()
    for o in range(1, N_TILE):
        pl.semaphore_signal(
            barrier, inc=1, device_id={"tile": (me + o) % N_TILE}, device_id_type=MESH
        )
    for o in range(1, N_DEPTH):
        pl.semaphore_signal(
            barrier, inc=1, device_id={"depth": (my_depth + o) % N_DEPTH}, device_id_type=MESH
        )

    running = jnp.int32(0)
    my_start = jnp.int32(0)
    my_position = jnp.int32(0)
    start_list = []
    for i in range(N_TILE):
        start_list.append(running)
        my_start = jnp.where(me == i, running, my_start)
        my_position = jnp.where(order[i] == me, i, my_position)
        running = running + counts[i]
    for o in range(N_TILE):
        tile = (me + o) % N_TILE
        position = jnp.int32(0)
        for i in range(N_TILE):
            position = jnp.where(order[i] == tile, i, position)
        rows[o] = (position - my_start) & (N_TILE - 1)

    def find(index, carry):
        wanted = index * N_TILE + my_position
        owner = jnp.int32(0)
        first = jnp.int32(0)
        for i in range(1, N_TILE):
            past = start_list[i] <= wanted
            owner = jnp.where(past, i, owner)
            first = jnp.where(past, start_list[i], first)
        found[index] = (((wanted - first) >> 4) & (GROUPS - 1)) * N_TILE + owner
        return carry

    lax.fori_loop(0, 2 * N_TILE, find, 0)
    my_flip = flips[me]
    slot = lax.broadcasted_iota(jnp.int32, (N_TILE, LANES), 0)
    sign = jnp.full((N_TILE, LANES), -1.0, jnp.float32)
    for s in range(N_TILE):
        flip = flips[order[(my_start + s) & (N_TILE - 1)]].astype(jnp.float32)
        sign = jnp.where(slot == s, 2.0 * flip - 1.0, sign)
    centers = [centers_ref[k] for k in range(KNOTS)]
    amps = [[amps_ref[c, k] * (1.0 if c == 3 else 0.5) for k in range(KNOTS)] for c in range(4)]

    def exchange(m, o):
        return pltpu.make_async_remote_copy(
            src_ref=send.at[m, o],
            dst_ref=recv.at[m * N_TILE + me],
            send_sem=send_sem.at[m, o],
            recv_sem=recv_sem.at[m, o],
            device_id={"tile": (me + o) % N_TILE},
            device_id_type=MESH,
        )

    copies = []
    for m in range(GROUPS):
        loads[m].wait()

        def column(chunk, carry):
            march(vox, img, sign, m * N_TILE, chunk, centers, amps)
            return carry

        lax.fori_loop(0, CHUNKS, column, 0)
        for o in range(N_TILE):
            image = img[:, rows[o], :]
            if o == 0:
                recv[m * N_TILE + me] = image
            else:
                send[m, o] = image
        if m == 0:
            pl.semaphore_wait(barrier, N_TILE + N_DEPTH - 2)
        for o in range(1, N_TILE):
            copy = exchange(m, o)
            copy.start()
            copies.append(copy)
    for copy in copies:
        copy.wait_recv()

    def layered(depth):
        by = depth // 2
        half = depth % 2
        parts = []
        for bx in range(4):
            low = found[by * 4 + bx]
            high = found[16 + by * 4 + bx]
            near = recv[jnp.where(my_flip == 1, high, low), pl.ds(half * 16, 16), :]
            far = recv[jnp.where(my_flip == 1, low, high), pl.ds(half * 16, 16), :]
            parts.append(over(near, far))
        return jnp.concatenate(parts, axis=0)

    shares = []
    for o in range(1, N_DEPTH):
        depth = (my_depth + o) % N_DEPTH
        dsend[o] = layered(depth)
        share = pltpu.make_async_remote_copy(
            src_ref=dsend.at[o],
            dst_ref=drecv.at[my_depth],
            send_sem=dsend_sem.at[o],
            recv_sem=drecv_sem.at[o],
            device_id={"depth": depth},
            device_id_type=MESH,
        )
        share.start()
        shares.append(share)
    drecv[my_depth] = layered(my_depth)
    for share in shares:
        share.wait_recv()

    blended = [jnp.zeros((16, LANES), jnp.float32) for bx in range(4)]
    for i in range(N_DEPTH):
        level = jnp.where(my_flip == 1, i, N_DEPTH - 1 - i)
        layer = drecv[level]
        blended = [over(layer[bx * 16 : bx * 16 + 16], blended[bx]) for bx in range(4)]
    lane_block = lax.broadcasted_iota(jnp.int32, (16, LANES), 1) // BLOCK
    for y in range(4):
        line = blended[0]
        for bx in range(4):
            shift = (bx - y) * BLOCK % LANES
            moved = pltpu.roll(blended[bx], shift, 1) if shift else blended[bx]
            line = moved if bx == 0 else jnp.where(lane_block == bx, moved, line)
        out[pl.ds(y, 16, stride=4), :] = line
    for copy in copies:
        copy.wait_send()
    for share in shares:
        share.wait_send()


def body(owned_blocks, slot_counts, brick_order, view_flip, tf_centers, tf_amps):
    smem = pl.BlockSpec(memory_space=pltpu.SMEM)
    image = pl.pallas_call(
        render,
        out_shape=jax.ShapeDtypeStruct((64, LANES), jnp.float32),
        in_specs=[smem] * 5 + [pl.BlockSpec(memory_space=pltpu.HBM)],
        out_specs=pl.BlockSpec(memory_space=pltpu.VMEM),
        scratch_shapes=[
            pltpu.VMEM((64, 32768), jnp.bfloat16),
            pltpu.VMEM((32, N_TILE, LANES), jnp.float32),
            pltpu.VMEM((GROUPS, N_TILE, 32, LANES), jnp.float32),
            pltpu.VMEM((64, 32, LANES), jnp.float32),
            pltpu.VMEM((N_DEPTH, 64, LANES), jnp.float32),
            pltpu.VMEM((N_DEPTH, 64, LANES), jnp.float32),
            pltpu.SMEM((N_TILE,), jnp.int32),
            pltpu.SMEM((N_TILE,), jnp.int32),
            pltpu.SMEM((2 * N_TILE,), jnp.int32),
            pltpu.SemaphoreType.DMA((GROUPS,)),
            pltpu.SemaphoreType.DMA((GROUPS, N_TILE)),
            pltpu.SemaphoreType.DMA((GROUPS, N_TILE)),
            pltpu.SemaphoreType.DMA((N_DEPTH,)),
            pltpu.SemaphoreType.DMA((N_DEPTH,)),
        ],
        compiler_params=pltpu.CompilerParams(
            collective_id=0, has_side_effects=True, vmem_limit_bytes=64000 * 1024
        ),
        name="render",
    )(
        slot_counts.reshape(N_TILE),
        brick_order.reshape(N_TILE),
        view_flip,
        tf_centers,
        tf_amps,
        owned_blocks.reshape(64, 32768),
    )
    return image.reshape(4, 16, LANES)


def solution(mesh):
    in_specs = (P("depth", "tile", None), P("depth", None), P("depth", None), P(), P(), P())
    out_specs = P(None, "depth", "tile")
    return jax.shard_map(body, mesh=mesh, in_specs=in_specs, out_specs=out_specs, check_vma=False)
```

time: 225 us -> 58.6 us (0.26)
  the two profiles are of different devices: /device:TPU:114 before, /device:TPU:1 now
where the time goes in v1:
time: 58.6 us; the launch traced here: 58.4 us
  Pallas kernels  57.1 us (97%)
  local copies, waits for them, and re-layouts  1.38 us (2%)
    pallas_call x1, Pallas kernels, body(): pl.pallas_call(render, out_shape=jax.ShapeDtypeStruct((64, LANES), jnp.fl...  57.1 us
    unnamed x1, local copies, waits for them, and re-layouts  1.38 us

profile of v1, /device:TPU:1, one launch (start us, length us, event | category | flops | bytes accessed | tf_op | source)
XLA Modules:
  0.0 58.4 jit_solution(12775693281827472565)
XLA Ops:
  0.0 57.1 %render.1 = f32[64,128]{1,0:T(8,128)} custom-call(s32[16]{0:T(128)} %bitcast.6, s32[16]{0:T(128)} %bitcast.7, s32[16]{0:T(128)} %flips.1, f32[8]{0:T(128)} %centers_ref.1, f32[4,8]{1,0:T(4,128)} %amps_ref.1, bf16[64,32768]{1,0:T(8,128)(2,1)} %bitcast.4), custom_call_target="tpu_custom_call" | custom-call | tf_op jit(solution)/shard_map/render/pallas_call | solution.py:209
  57.1 1.4 %copy.8 = f32[4,16,128]{2,1,0:T(8,128)} copy(f32[4,16,128]{2,1,0:T(8,128)} %bitcast.5) | data formatting | bytes 65536

commit v2 on v1

--- a/solution.py
+++ b/solution.py
@@ -17,41 +17,95 @@
 PIXELS = BLOCK * BLOCK
 CHUNKS = PIXELS // LANES
 STEP = 1.5 / 512
-
-
-def march(vox, img, sign, row0, chunk, centers, amps):
-    step_sign = sign * STEP
-
-    def body(z, carry):
+HALF = 8
+WIDE = 256
+LOG2E = 1.4426950408889634
+SPAN = 4
+SPANS = BLOCK // SPAN
+PAIRS = PIXELS // WIDE
+
+
+def split(x):
+    high = x.astype(jnp.bfloat16)
+    return high, x - high.astype(jnp.float32)
+
+
+def set_mix(mix, centers, amps):
+    row = lax.broadcasted_iota(jnp.int32, (HALF, KNOTS * HALF), 0)
+    column = lax.broadcasted_iota(jnp.int32, (HALF, KNOTS * HALF), 1)
+    same = column % HALF == row
+    block = column // HALF
+    center = jnp.zeros(row.shape, jnp.float32)
+    for k in range(KNOTS):
+        center = jnp.where(block == k, centers[k], center)
+    fall = jnp.exp(center * center * -4.0)
+    for c in range(4):
+        value = jnp.zeros(row.shape, jnp.float32)
+        for k in range(KNOTS):
+            value = jnp.where(block == k, amps[c][k], value)
+        value = jnp.where(same, value * fall * (LOG2E if c == 3 else 0.5), 0.0)
+        high, rest = split(value)
+        parts = [high.astype(jnp.float32)] * 2 + [rest]
+        mix[c * HALF : (c + 1) * HALF, :] = jnp.concatenate(parts, axis=1).astype(jnp.bfloat16)
+
+
+def set_fields(vox, mix, fields, slopes, index):
+    index = jnp.minimum(index, GROUPS * PAIRS * SPANS - 1)
+    row = pl.multiple_of(index // (PAIRS * SPANS) * N_TILE, N_TILE)
+    first = index % SPANS * (SPAN * PIXELS) + index // SPANS % PAIRS * WIDE
+    for u in range(SPAN):
+        lane = pl.multiple_of(first + u * PIXELS, WIDE)
+        both = vox[pl.ds(row, N_TILE), pl.ds(lane, WIDE)].astype(jnp.float32)
+        for h in range(2):
+            value = both[h * HALF : (h + 1) * HALF]
+            slope = value * (4.0 * LOG2E)
+            bump = jnp.concatenate([jnp.exp2(value * (s - slope)) for s in slopes], axis=0)
+            high, rest = split(bump)
+            parts = jnp.concatenate([high, rest.astype(jnp.bfloat16), high], axis=0)
+            fields[u, h] = jnp.dot(mix[...], parts, preferred_element_type=jnp.float32)
+
+
+def advance(fields, step_sign, carry):
+    for u in range(SPAN):
         total, held, red, green, blue = carry
-        lane = pl.multiple_of(z * PIXELS + chunk * LANES, LANES)
-        value = vox[pl.ds(row0, N_TILE), pl.ds(lane, LANES)].astype(jnp.float32)
-        fields = [None] * 4
-        for k in range(KNOTS):
-            off = value - centers[k]
-            bump = jnp.exp(off * off * -4.0)
-            for c in range(4):
-                term = amps[c][k] * bump
-                fields[c] = term if k == 0 else fields[c] + term
-        total = total + jnp.log(1.0 + jnp.exp(fields[3]))
-        now = jnp.exp(total * step_sign)
+        field = [
+            jnp.concatenate([fields[u, h, c * HALF : (c + 1) * HALF] for h in range(2)], axis=0)
+            for c in range(4)
+        ]
+        total = total + jnp.log(1.0 + jnp.exp2(field[3]))
+        now = jnp.exp2(total * step_sign)
         weight = held - now
-        red = red + weight * jnp.tanh(fields[0])
-        green = green + weight * jnp.tanh(fields[1])
-        blue = blue + weight * jnp.tanh(fields[2])
-        return total, now, red, green, blue
-
-    zero = jnp.zeros((N_TILE, LANES), jnp.float32)
+        red = red + weight * jnp.tanh(field[0])
+        green = green + weight * jnp.tanh(field[1])
+        blue = blue + weight * jnp.tanh(field[2])
+        carry = total, now, red, green, blue
+    return carry
+
+
+def march(vox, img, mix, even, odd, slopes, sign, group, pair):
+    step_sign = sign * (STEP * LOG2E)
+    base = (group * PAIRS + pair) * SPANS
+
+    def body(i, carry):
+        set_fields(vox, mix, odd, slopes, base + 2 * i + 1)
+        carry = advance(even, step_sign, carry)
+        set_fields(vox, mix, even, slopes, base + 2 * i + 2)
+        return advance(odd, step_sign, carry)
+
+    zero = jnp.zeros((N_TILE, WIDE), jnp.float32)
     total, held, red, green, blue = lax.fori_loop(
-        0, BLOCK, body, (zero, zero + 1.0, zero, zero, zero), unroll=4
+        0, SPANS // 2, body, (zero, zero + 1.0, zero, zero, zero)
     )
-    through = jnp.exp(total * -STEP)
+    through = jnp.exp2(total * (-STEP * LOG2E))
     scale = jnp.where(sign < 0.0, 0.5, -0.5 * through)
-    half = chunk // 4
-    quarter = chunk % 4
-    for c, colour in enumerate((red, green, blue)):
-        img[half * 16 + c * 4 + quarter] = scale * ((1.0 - held) + colour)
-    img[half * 16 + 12 + quarter] = 1.0 - through
+    values = [scale * ((1.0 - held) + colour) for colour in (red, green, blue)]
+    values.append(1.0 - through)
+    half = pair // 2
+    for c in range(4):
+        for side in range(2):
+            quarter = pair % 2 * 2 + side
+            row = pl.multiple_of((half * 16 + c * 4 + quarter) * N_TILE, N_TILE)
+            img[pl.ds(row, N_TILE), :] = values[c][:, side * LANES : (side + 1) * LANES]
 
 
 def over(nearer, farther):
@@ -63,7 +117,7 @@
 
 def render(
     counts, order, flips, centers_ref, amps_ref, blocks, out,
-    vox, img, send, recv, dsend, drecv, starts, rows, found,
+    vox, img, mix, even, odd, send, recv, dsend, drecv, starts, rows, found,
     load_sem, send_sem, recv_sem, dsend_sem, drecv_sem,
 ):
     me = lax.axis_index("tile")
@@ -113,13 +167,15 @@
 
     lax.fori_loop(0, 2 * N_TILE, find, 0)
     my_flip = flips[me]
-    slot = lax.broadcasted_iota(jnp.int32, (N_TILE, LANES), 0)
-    sign = jnp.full((N_TILE, LANES), -1.0, jnp.float32)
+    slot = lax.broadcasted_iota(jnp.int32, (N_TILE, WIDE), 0)
+    sign = jnp.full((N_TILE, WIDE), -1.0, jnp.float32)
     for s in range(N_TILE):
         flip = flips[order[(my_start + s) & (N_TILE - 1)]].astype(jnp.float32)
         sign = jnp.where(slot == s, 2.0 * flip - 1.0, sign)
     centers = [centers_ref[k] for k in range(KNOTS)]
-    amps = [[amps_ref[c, k] * (1.0 if c == 3 else 0.5) for k in range(KNOTS)] for c in range(4)]
+    amps = [[amps_ref[c, k] for k in range(KNOTS)] for c in range(4)]
+    set_mix(mix, centers, amps)
+    slopes = [center * (8.0 * LOG2E) for center in centers]
 
     def exchange(m, o):
         return pltpu.make_async_remote_copy(
@@ -133,15 +189,23 @@
 
     copies = []
     for m in range(GROUPS):
-        loads[m].wait()
-
-        def column(chunk, carry):
-            march(vox, img, sign, m * N_TILE, chunk, centers, amps)
+        if m == 0:
+            loads[0].wait()
+            set_fields(vox, mix, even, slopes, 0)
+
+        def column(pair, carry):
+            if m + 1 < GROUPS:
+
+                @pl.when(pair == PAIRS - 1)
+                def _():
+                    loads[m + 1].wait()
+
+            march(vox, img, mix, even, odd, slopes, sign, m, pair)
             return carry
 
-        lax.fori_loop(0, CHUNKS, column, 0)
+        lax.fori_loop(0, PAIRS, column, 0)
         for o in range(N_TILE):
-            image = img[:, rows[o], :]
+            image = img[pl.ds(rows[o], 32, stride=N_TILE), :]
             if o == 0:
                 recv[m * N_TILE + me] = image
             else:
@@ -213,7 +277,10 @@
         out_specs=pl.BlockSpec(memory_space=pltpu.VMEM),
         scratch_shapes=[
             pltpu.VMEM((64, 32768), jnp.bfloat16),
-            pltpu.VMEM((32, N_TILE, LANES), jnp.float32),
+            pltpu.VMEM((32 * N_TILE, LANES), jnp.float32),
+            pltpu.VMEM((4 * HALF, 3 * KNOTS * HALF), jnp.bfloat16),
+            pltpu.VMEM((SPAN, 2, 4 * HALF, WIDE), jnp.float32),
+            pltpu.VMEM((SPAN, 2, 4 * HALF, WIDE), jnp.float32),
             pltpu.VMEM((GROUPS, N_TILE, 32, LANES), jnp.float32),
             pltpu.VMEM((64, 32, LANES), jnp.float32),
             pltpu.VMEM((N_DEPTH, 64, LANES), jnp.float32),

time: 58.6 us -> 52.8 us (0.901)
  Pallas kernels: 57.1 us -> 51.2 us
    pallas_call x1, Pallas kernels: 57.1 us -> 51.2 us  [body(): pl.pallas_call(render, out_shape=jax.ShapeDtypeStruct((64, LANES), jnp.fl...]
where the time goes in v2:
time: 52.8 us; the launch traced here: 52.6 us
  Pallas kernels  51.2 us (97%)
  local copies, waits for them, and re-layouts  1.38 us (3%)
    pallas_call x1, Pallas kernels, body(): pl.pallas_call(render, out_shape=jax.ShapeDtypeStruct((64, LANES), jnp.fl...  51.2 us
    unnamed x1, local copies, waits for them, and re-layouts  1.38 us

profile of v2, /device:TPU:1, one launch (start us, length us, event | category | flops | bytes accessed | tf_op | source)
XLA Modules:
  0.0 52.6 jit_solution(11735885297261512252)
XLA Ops:
  0.0 51.2 %render.1 = f32[64,128]{1,0:T(8,128)} custom-call(s32[16]{0:T(128)} %bitcast.6, s32[16]{0:T(128)} %bitcast.7, s32[16]{0:T(128)} %flips.1, f32[8]{0:T(128)} %centers_ref.1, f32[4,8]{1,0:T(4,128)} %amps_ref.1, bf16[64,32768]{1,0:T(8,128)(2,1)} %bitcast.4), custom_call_target="tpu_custom_call" | custom-call | tf_op jit(solution)/shard_map/render/pallas_call | solution.py:273
  51.2 1.4 %copy.8 = f32[4,16,128]{2,1,0:T(8,128)} copy(f32[4,16,128]{2,1,0:T(8,128)} %bitcast.5) | data formatting | bytes 65536

commit v3 on v2

v3 whole, which is shorter than its diff:
```python
import functools

import jax
import jax.numpy as jnp
from jax import lax
from jax.experimental import pallas as pl
from jax.experimental.pallas import tpu as pltpu
from jax.sharding import PartitionSpec as P

MESH = pl.DeviceIdType.MESH
BLOCK = 32
KNOTS = 8
N_TILE = 16
N_DEPTH = 8
GROUPS = 4
LANES = 128
PIXELS = BLOCK * BLOCK
STEP = 1.5 / 512
HALF = 8
WIDE = 256
LOG2E = 1.4426950408889634
SPAN = 8
SPANS = BLOCK // SPAN
QUARTERS = PIXELS // WIDE


def split(x):
    high = x.astype(jnp.bfloat16)
    return high, x - high.astype(jnp.float32)


def set_mix(mix, centers, amps):
    row = lax.broadcasted_iota(jnp.int32, (HALF, KNOTS * HALF), 0)
    column = lax.broadcasted_iota(jnp.int32, (HALF, KNOTS * HALF), 1)
    same = column % HALF == row
    block = column // HALF
    center = jnp.zeros(row.shape, jnp.float32)
    for k in range(KNOTS):
        center = jnp.where(block == k, centers[k], center)
    fall = jnp.exp(center * center * -4.0)
    for c in range(4):
        value = jnp.zeros(row.shape, jnp.float32)
        for k in range(KNOTS):
            value = jnp.where(block == k, amps[c][k], value)
        value = jnp.where(same, value * fall * (LOG2E if c == 3 else 0.5), 0.0)
        high, rest = split(value)
        parts = [high.astype(jnp.float32)] * 2 + [rest]
        mix[c * HALF : (c + 1) * HALF, :] = jnp.concatenate(parts, axis=1).astype(jnp.bfloat16)


def set_fields(vox, mix, fields, slopes, index):
    index = jnp.minimum(index, QUARTERS * GROUPS * SPANS - 1)
    row = pl.multiple_of(index // SPANS % GROUPS * N_TILE, N_TILE)
    first = index % SPANS * (SPAN * PIXELS) + index // (SPANS * GROUPS) * WIDE
    for u in range(SPAN):
        lane = pl.multiple_of(first + u * PIXELS, WIDE)
        both = vox[pl.ds(row, N_TILE), pl.ds(lane, WIDE)].astype(jnp.float32)
        for h in range(2):
            value = both[h * HALF : (h + 1) * HALF]
            slope = value * (4.0 * LOG2E)
            bump = jnp.concatenate([jnp.exp2(value * (s - slope)) for s in slopes], axis=0)
            high, rest = split(bump)
            parts = jnp.concatenate([high, rest.astype(jnp.bfloat16), high], axis=0)
            fields[u, h] = jnp.dot(mix[...], parts, preferred_element_type=jnp.float32)


def advance(fields, step_sign, carry):
    for u in range(SPAN):
        total, held, red, green, blue = carry
        field = [
            jnp.concatenate([fields[u, h, c * HALF : (c + 1) * HALF] for h in range(2)], axis=0)
            for c in range(4)
        ]
        total = total + jnp.log(1.0 + jnp.exp2(field[3]))
        now = jnp.exp2(total * step_sign)
        weight = held - now
        red = red + weight * jnp.tanh(field[0])
        green = green + weight * jnp.tanh(field[1])
        blue = blue + weight * jnp.tanh(field[2])
        carry = total, now, red, green, blue
    return carry


def march(vox, img, mix, even, odd, slopes, sign, quarter, group):
    step_sign = sign * (STEP * LOG2E)
    base = (quarter * GROUPS + group) * SPANS

    def body(i, carry):
        set_fields(vox, mix, odd, slopes, base + 2 * i + 1)
        carry = advance(even, step_sign, carry)
        set_fields(vox, mix, even, slopes, base + 2 * i + 2)
        return advance(odd, step_sign, carry)

    zero = jnp.zeros((N_TILE, WIDE), jnp.float32)
    total, held, red, green, blue = lax.fori_loop(
        0, SPANS // 2, body, (zero, zero + 1.0, zero, zero, zero)
    )
    through = jnp.exp2(total * (-STEP * LOG2E))
    scale = jnp.where(sign < 0.0, 0.5, -0.5 * through)
    values = [scale * ((1.0 - held) + colour) for colour in (red, green, blue)]
    values.append(1.0 - through)
    for c in range(4):
        for side in range(2):
            row = (side * 4 + c) * N_TILE
            img[row : row + N_TILE, :] = values[c][:, side * LANES : (side + 1) * LANES]


def over(nearer, farther):
    clear = 1.0 - nearer
    left = jnp.broadcast_to(clear[3:4], (4, LANES))
    right = jnp.broadcast_to(clear[7:8], (4, LANES))
    return nearer + jnp.concatenate([left, right], axis=0) * farther


def render(
    counts, order, flips, centers_ref, amps_ref, blocks, out,
    vox, img, mix, even, odd, send, recv0, recv1, recv2, recv3, dsend, drecv, starts, rows, found,
    load_sem, send_sem, recv_sem, dsend_sem, drecv_sem,
):
    me = lax.axis_index("tile")
    my_depth = lax.axis_index("depth")
    recv = (recv0, recv1, recv2, recv3)

    def load(m):
        part = pl.ds(pl.multiple_of(m * N_TILE, N_TILE), N_TILE)
        return pltpu.make_async_copy(blocks.at[part, :], vox.at[part, :], load_sem.at[m])

    for m in range(GROUPS):
        load(m).start()
    barrier = pltpu.get_barrier_semaphore()
    for o in range(1, N_TILE):
        pl.semaphore_signal(
            barrier, inc=1, device_id={"tile": (me + o) % N_TILE}, device_id_type=MESH
        )
    for o in range(1, N_DEPTH):
        pl.semaphore_signal(
            barrier, inc=1, device_id={"depth": (my_depth + o) % N_DEPTH}, device_id_type=MESH
        )

    running = jnp.int32(0)
    my_start = jnp.int32(0)
    my_position = jnp.int32(0)
    for i in range(N_TILE):
        starts[i] = running
        my_start = jnp.where(me == i, running, my_start)
        my_position = jnp.where(order[i] == me, i, my_position)
        running = running + counts[i]
    for o in range(N_TILE):
        tile = (me + o) % N_TILE
        position = jnp.int32(0)
        for i in range(N_TILE):
            position = jnp.where(order[i] == tile, i, position)
        rows[o] = (position - my_start) & (N_TILE - 1)

    def find(block, carry):
        for u in range(8):
            index = block * 8 + u
            wanted = index * N_TILE + my_position
            owner = jnp.int32(0)
            for hop in (8, 4, 2, 1):
                owner = jnp.where(starts[owner + hop] <= wanted, owner + hop, owner)
            depth = ((wanted - starts[owner]) >> 4) & (GROUPS - 1)
            found[index] = owner * GROUPS + depth
        return carry

    lax.fori_loop(0, N_TILE // 4, find, 0)
    my_flip = flips[me]
    slot = lax.broadcasted_iota(jnp.int32, (N_TILE, WIDE), 0)
    sign = jnp.full((N_TILE, WIDE), -1.0, jnp.float32)
    for s in range(N_TILE):
        flip = flips[order[(my_start + s) & (N_TILE - 1)]].astype(jnp.float32)
        sign = jnp.where(slot == s, 2.0 * flip - 1.0, sign)
    centers = [centers_ref[k] for k in range(KNOTS)]
    amps = [[amps_ref[c, k] for k in range(KNOTS)] for c in range(4)]
    set_mix(mix, centers, amps)
    slopes = [center * (8.0 * LOG2E) for center in centers]

    def exchange(q, o):
        return pltpu.make_async_remote_copy(
            src_ref=send.at[q, o],
            dst_ref=recv[q].at[pl.ds(me * GROUPS, GROUPS)],
            send_sem=send_sem.at[q, o],
            recv_sem=recv_sem.at[q, o],
            device_id={"tile": (me + o) % N_TILE},
            device_id_type=MESH,
        )

    def piece(m, o):
        return pltpu.make_async_remote_copy(
            src_ref=send.at[QUARTERS - 1, o, m],
            dst_ref=recv[QUARTERS - 1].at[me * GROUPS + m],
            send_sem=send_sem.at[QUARTERS - 1 + m, o],
            recv_sem=recv_sem.at[QUARTERS - 1 + m, o],
            device_id={"tile": (me + o) % N_TILE},
            device_id_type=MESH,
        )

    def share(q, by):
        return pltpu.make_async_remote_copy(
            src_ref=dsend.at[q, by],
            dst_ref=drecv.at[q % 2, my_depth],
            send_sem=dsend_sem.at[q, by],
            recv_sem=drecv_sem.at[q % 2, my_depth],
            device_id={"depth": 2 * by + q // 2},
            device_id_type=MESH,
        )

    def layers(q, by):
        parts = []
        for bx in range(4):
            low = found[by * 4 + bx]
            high = found[16 + by * 4 + bx]
            near = recv[q][jnp.where(my_flip == 1, high, low)]
            far = recv[q][jnp.where(my_flip == 1, low, high)]
            parts.append(over(near, far))
        return jnp.stack(parts, axis=0)

    def share_out(q):
        for j in range(1, 4):
            by = (my_depth // 2 + j) % 4
            dsend[q, by] = layers(q, by)
            share(q, by).start()
        by = my_depth // 2
        mine = layers(q, by)

        @pl.when(my_depth % 2 == q // 2)
        def _():
            drecv[q % 2, my_depth] = mine

        @pl.when(my_depth % 2 != q // 2)
        def _():
            dsend[q, by] = mine
            share(q, by).start()

    load(0).wait()
    set_fields(vox, mix, even, slopes, 0)
    for q in range(QUARTERS):

        def group(m, carry):
            if q == 0:

                @pl.when(m + 1 < GROUPS)
                def _():
                    load(m + 1).wait()

            march(vox, img, mix, even, odd, slopes, sign, q, m)
            for o in range(N_TILE):
                image = img[pl.ds(rows[o], 8, stride=N_TILE), :]
                if o == 0:
                    recv[q][me * GROUPS + m] = image
                else:
                    send[q, o, m] = image
            if q == QUARTERS - 1:
                for o in range(1, N_TILE):
                    piece(m, o).start()
            return carry

        lax.fori_loop(0, GROUPS, group, 0)
        if q == 0:
            pl.semaphore_wait(barrier, N_TILE + N_DEPTH - 2)
        if q < QUARTERS - 1:
            for o in range(1, N_TILE):
                exchange(q, o).start()
        if q > 0:
            for o in range(1, N_TILE):
                exchange(q - 1, o).wait_recv()
            share_out(q - 1)
    for m in range(GROUPS):
        for o in range(1, N_TILE):
            piece(m, o).wait_recv()
    share_out(QUARTERS - 1)

    def arrived(side, o):
        source = (my_depth + o) % N_DEPTH
        return pltpu.make_async_remote_copy(
            src_ref=dsend.at[side, 0],
            dst_ref=drecv.at[side, source],
            send_sem=dsend_sem.at[side, 0],
            recv_sem=drecv_sem.at[side, source],
            device_id={"depth": source},
            device_id_type=MESH,
        )

    for side in range(2):
        for o in range(1, N_DEPTH):
            arrived(side, o).wait_recv()
    lane_block = lax.broadcasted_iota(jnp.int32, (8, LANES), 1) // BLOCK
    for side in range(2):
        blended = [jnp.zeros((8, LANES), jnp.float32) for bx in range(4)]
        for i in range(N_DEPTH):
            level = jnp.where(my_flip == 1, i, N_DEPTH - 1 - i)
            layer = drecv[side, level]
            blended = [over(layer[bx], blended[bx]) for bx in range(4)]
        for y in range(4):
            line = blended[0]
            for bx in range(4):
                shift = (bx - y) * BLOCK % LANES
                moved = pltpu.roll(blended[bx], shift, 1) if shift else blended[bx]
                line = moved if bx == 0 else jnp.where(lane_block == bx, moved, line)
            for half in range(2):
                row = side * 8 + half * 4 + y
                out[pl.ds(row, 4, stride=16), :] = line[half * 4 : half * 4 + 4]

    for o in range(1, N_TILE):
        for q in range(QUARTERS - 1):
            exchange(q, o).wait_send()
        for m in range(GROUPS):
            piece(m, o).wait_send()
    for q in range(QUARTERS):
        for j in range(1, 4):
            share(q, (my_depth // 2 + j) % 4).wait_send()

        @pl.when(my_depth % 2 != q // 2)
        def _():
            share(q, my_depth // 2).wait_send()


def body(owned_blocks, slot_counts, brick_order, view_flip, tf_centers, tf_amps):
    smem = pl.BlockSpec(memory_space=pltpu.SMEM)
    image = pl.pallas_call(
        render,
        out_shape=jax.ShapeDtypeStruct((64, LANES), jnp.float32),
        in_specs=[smem] * 5 + [pl.BlockSpec(memory_space=pltpu.HBM)],
        out_specs=pl.BlockSpec(memory_space=pltpu.VMEM),
        scratch_shapes=[
            pltpu.VMEM((64, 32768), jnp.bfloat16),
            pltpu.VMEM((8 * N_TILE, LANES), jnp.float32),
            pltpu.VMEM((4 * HALF, 3 * KNOTS * HALF), jnp.bfloat16),
            pltpu.VMEM((SPAN, 2, 4 * HALF, WIDE), jnp.float32),
            pltpu.VMEM((SPAN, 2, 4 * HALF, WIDE), jnp.float32),
            pltpu.VMEM((QUARTERS, N_TILE, GROUPS, 8, LANES), jnp.float32),
            pltpu.VMEM((N_TILE * GROUPS, 8, LANES), jnp.float32),
            pltpu.VMEM((N_TILE * GROUPS, 8, LANES), jnp.float32),
            pltpu.VMEM((N_TILE * GROUPS, 8, LANES), jnp.float32),
            pltpu.VMEM((N_TILE * GROUPS, 8, LANES), jnp.float32),
            pltpu.VMEM((QUARTERS, 4, 4, 8, LANES), jnp.float32),
            pltpu.VMEM((2, N_DEPTH, 4, 8, LANES), jnp.float32),
            pltpu.SMEM((N_TILE,), jnp.int32),
            pltpu.SMEM((N_TILE,), jnp.int32),
            pltpu.SMEM((2 * N_TILE,), jnp.int32),
            pltpu.SemaphoreType.DMA((GROUPS,)),
            pltpu.SemaphoreType.DMA((QUARTERS - 1 + GROUPS, N_TILE)),
            pltpu.SemaphoreType.DMA((QUARTERS - 1 + GROUPS, N_TILE)),
            pltpu.SemaphoreType.DMA((QUARTERS, 4)),
            pltpu.SemaphoreType.DMA((2, N_DEPTH)),
        ],
        compiler_params=pltpu.CompilerParams(
            collective_id=0, has_side_effects=True, vmem_limit_bytes=64000 * 1024
        ),
        name="render",
    )(
        slot_counts.reshape(N_TILE),
        brick_order.reshape(N_TILE),
        view_flip,
        tf_centers,
        tf_amps,
        owned_blocks.reshape(64, 32768),
    )
    return image.reshape(4, 16, LANES)


def solution(mesh):
    in_specs = (P("depth", "tile", None), P("depth", None), P("depth", None), P(), P(), P())
    out_specs = P(None, "depth", "tile")
    return jax.shard_map(body, mesh=mesh, in_specs=in_specs, out_specs=out_specs, check_vma=False)
```

time: 52.8 us -> 50.1 us (0.949)
  Pallas kernels: 51.2 us -> 48.5 us
    pallas_call x1, Pallas kernels: 51.2 us -> 48.5 us  [body(): pl.pallas_call(render, out_shape=jax.ShapeDtypeStruct((64, LANES), jnp.fl...]
where the time goes in v3:
time: 50.1 us; the launch traced here: 49.9 us
  Pallas kernels  48.5 us (97%)
  local copies, waits for them, and re-layouts  1.38 us (3%)
    pallas_call x1, Pallas kernels, body(): pl.pallas_call(render, out_shape=jax.ShapeDtypeStruct((64, LANES), jnp.fl...  48.5 us
    unnamed x1, local copies, waits for them, and re-layouts  1.38 us

profile of v3, /device:TPU:1, one launch (start us, length us, event | category | flops | bytes accessed | tf_op | source)
XLA Modules:
  0.0 49.9 jit_solution(1745513702472740464)
XLA Ops:
  0.0 48.5 %render.1 = f32[64,128]{1,0:T(8,128)} custom-call(s32[16]{0:T(128)} %bitcast.6, s32[16]{0:T(128)} %bitcast.7, s32[16]{0:T(128)} %flips.1, f32[8]{0:T(128)} %centers_ref.1, f32[4,8]{1,0:T(4,128)} %amps_ref.1, bf16[64,32768]{1,0:T(8,128)(2,1)} %bitcast.4), custom_call_target="tpu_custom_call" | custom-call | tf_op jit(solution)/shard_map/render/pallas_call | solution.py:320
  48.6 1.4 %copy.8 = f32[4,16,128]{2,1,0:T(8,128)} copy(f32[4,16,128]{2,1,0:T(8,128)} %bitcast.5) | data formatting | bytes 65536

commit v4 on v3

--- a/solution.py
+++ b/solution.py
@@ -19,7 +19,7 @@
 HALF = 8
 WIDE = 256
 LOG2E = 1.4426950408889634
-SPAN = 8
+SPAN = 16
 SPANS = BLOCK // SPAN
 QUARTERS = PIXELS // WIDE
 
@@ -71,7 +71,7 @@
             jnp.concatenate([fields[u, h, c * HALF : (c + 1) * HALF] for h in range(2)], axis=0)
             for c in range(4)
         ]
-        total = total + jnp.log(1.0 + jnp.exp2(field[3]))
+        total = total + lax.log2(1.0 + jnp.exp2(field[3]))
         now = jnp.exp2(total * step_sign)
         weight = held - now
         red = red + weight * jnp.tanh(field[0])
@@ -82,7 +82,7 @@
 
 
 def march(vox, img, mix, even, odd, slopes, sign, quarter, group):
-    step_sign = sign * (STEP * LOG2E)
+    step_sign = sign * STEP
     base = (quarter * GROUPS + group) * SPANS
 
     def body(i, carry):
@@ -95,7 +95,7 @@
     total, held, red, green, blue = lax.fori_loop(
         0, SPANS // 2, body, (zero, zero + 1.0, zero, zero, zero)
     )
-    through = jnp.exp2(total * (-STEP * LOG2E))
+    through = jnp.exp2(total * -STEP)
     scale = jnp.where(sign < 0.0, 0.5, -0.5 * through)
     values = [scale * ((1.0 - held) + colour) for colour in (red, green, blue)]
     values.append(1.0 - through)
@@ -232,6 +232,14 @@
             dsend[q, by] = mine
             share(q, by).start()
 
+    def shared(q):
+        for j in range(1, 4):
+            share(q, (my_depth // 2 + j) % 4).wait_send()
+
+        @pl.when(my_depth % 2 != q // 2)
+        def _():
+            share(q, my_depth // 2).wait_send()
+
     load(0).wait()
     set_fields(vox, mix, even, slopes, 0)
     for q in range(QUARTERS):
@@ -265,10 +273,18 @@
             for o in range(1, N_TILE):
                 exchange(q - 1, o).wait_recv()
             share_out(q - 1)
+    for o in range(1, N_TILE):
+        for q in range(QUARTERS - 1):
+            exchange(q, o).wait_send()
+    for q in range(QUARTERS - 1):
+        shared(q)
     for m in range(GROUPS):
         for o in range(1, N_TILE):
             piece(m, o).wait_recv()
     share_out(QUARTERS - 1)
+    for m in range(GROUPS):
+        for o in range(1, N_TILE):
+            piece(m, o).wait_send()
 
     def arrived(side, o):
         source = (my_depth + o) % N_DEPTH
@@ -300,19 +316,7 @@
             for half in range(2):
                 row = side * 8 + half * 4 + y
                 out[pl.ds(row, 4, stride=16), :] = line[half * 4 : half * 4 + 4]
-
-    for o in range(1, N_TILE):
-        for q in range(QUARTERS - 1):
-            exchange(q, o).wait_send()
-        for m in range(GROUPS):
-            piece(m, o).wait_send()
-    for q in range(QUARTERS):
-        for j in range(1, 4):
-            share(q, (my_depth // 2 + j) % 4).wait_send()
-
-        @pl.when(my_depth % 2 != q // 2)
-        def _():
-            share(q, my_depth // 2).wait_send()
+    shared(QUARTERS - 1)
 
 
 def body(owned_blocks, slot_counts, brick_order, view_flip, tf_centers, tf_amps):

time: 50.1 us -> 48.6 us (0.970)
  Pallas kernels: 48.5 us -> 47 us
    pallas_call x1, Pallas kernels: 48.5 us -> 47 us  [body(): pl.pallas_call(render, out_shape=jax.ShapeDtypeStruct((64, LANES), jnp.fl...]
where the time goes in v4:
time: 48.6 us; the launch traced here: 48.4 us
  Pallas kernels  47 us (97%)
  local copies, waits for them, and re-layouts  1.38 us (3%)
    pallas_call x1, Pallas kernels, body(): pl.pallas_call(render, out_shape=jax.ShapeDtypeStruct((64, LANES), jnp.fl...  47 us
    unnamed x1, local copies, waits for them, and re-layouts  1.38 us

profile of v4, /device:TPU:1, one launch (start us, length us, event | category | flops | bytes accessed | tf_op | source)
XLA Modules:
  0.0 48.4 jit_solution(117667701718539273)
XLA Ops:
  0.0 47.0 %render.1 = f32[64,128]{1,0:T(8,128)} custom-call(s32[16]{0:T(128)} %bitcast.6, s32[16]{0:T(128)} %bitcast.7, s32[16]{0:T(128)} %flips.1, f32[8]{0:T(128)} %centers_ref.1, f32[4,8]{1,0:T(4,128)} %amps_ref.1, bf16[64,32768]{1,0:T(8,128)(2,1)} %bitcast.4), custom_call_target="tpu_custom_call" | custom-call | tf_op jit(solution)/shard_map/render/pallas_call | solution.py:324
  47.0 1.4 %copy.8 = f32[4,16,128]{2,1,0:T(8,128)} copy(f32[4,16,128]{2,1,0:T(8,128)} %bitcast.5) | data formatting | bytes 65536

commit v5 on v4

--- a/solution.py
+++ b/solution.py
@@ -20,13 +20,9 @@
 WIDE = 256
 LOG2E = 1.4426950408889634
 SPAN = 16
+JOIN = 4
 SPANS = BLOCK // SPAN
 QUARTERS = PIXELS // WIDE
-
-
-def split(x):
-    high = x.astype(jnp.bfloat16)
-    return high, x - high.astype(jnp.float32)
 
 
 def set_mix(mix, centers, amps):
@@ -43,25 +39,32 @@
         for k in range(KNOTS):
             value = jnp.where(block == k, amps[c][k], value)
         value = jnp.where(same, value * fall * (LOG2E if c == 3 else 0.5), 0.0)
-        high, rest = split(value)
-        parts = [high.astype(jnp.float32)] * 2 + [rest]
-        mix[c * HALF : (c + 1) * HALF, :] = jnp.concatenate(parts, axis=1).astype(jnp.bfloat16)
+        mix[c * HALF : (c + 1) * HALF, :] = value
 
 
 def set_fields(vox, mix, fields, slopes, index):
     index = jnp.minimum(index, QUARTERS * GROUPS * SPANS - 1)
     row = pl.multiple_of(index // SPANS % GROUPS * N_TILE, N_TILE)
     first = index % SPANS * (SPAN * PIXELS) + index // (SPANS * GROUPS) * WIDE
-    for u in range(SPAN):
-        lane = pl.multiple_of(first + u * PIXELS, WIDE)
-        both = vox[pl.ds(row, N_TILE), pl.ds(lane, WIDE)].astype(jnp.float32)
+    for start in range(0, SPAN, JOIN):
+        halves = ([], [])
+        for u in range(start, start + JOIN):
+            lane = pl.multiple_of(first + u * PIXELS, WIDE)
+            both = vox[pl.ds(row, N_TILE), pl.ds(lane, WIDE)].astype(jnp.float32)
+            for h in range(2):
+                value = both[h * HALF : (h + 1) * HALF]
+                slope = value * (4.0 * LOG2E)
+                bumps = [jnp.exp2(value * (s - slope)) for s in slopes]
+                halves[h].append(jnp.concatenate(bumps, axis=0))
         for h in range(2):
-            value = both[h * HALF : (h + 1) * HALF]
-            slope = value * (4.0 * LOG2E)
-            bump = jnp.concatenate([jnp.exp2(value * (s - slope)) for s in slopes], axis=0)
-            high, rest = split(bump)
-            parts = jnp.concatenate([high, rest.astype(jnp.bfloat16), high], axis=0)
-            fields[u, h] = jnp.dot(mix[...], parts, preferred_element_type=jnp.float32)
+            mixed = jnp.dot(
+                mix[...],
+                jnp.concatenate(halves[h], axis=1),
+                preferred_element_type=jnp.float32,
+                precision=lax.Precision.HIGH,
+            )
+            for u in range(JOIN):
+                fields[start + u, h] = mixed[:, u * WIDE : (u + 1) * WIDE]
 
 
 def advance(fields, step_sign, carry):
@@ -329,7 +332,7 @@
         scratch_shapes=[
             pltpu.VMEM((64, 32768), jnp.bfloat16),
             pltpu.VMEM((8 * N_TILE, LANES), jnp.float32),
-            pltpu.VMEM((4 * HALF, 3 * KNOTS * HALF), jnp.bfloat16),
+            pltpu.VMEM((4 * HALF, KNOTS * HALF), jnp.float32),
             pltpu.VMEM((SPAN, 2, 4 * HALF, WIDE), jnp.float32),
             pltpu.VMEM((SPAN, 2, 4 * HALF, WIDE), jnp.float32),
             pltpu.VMEM((QUARTERS, N_TILE, GROUPS, 8, LANES), jnp.float32),

time: 48.6 us -> 47.6 us (0.979)
  Pallas kernels: 47 us -> 46 us
    pallas_call x1, Pallas kernels: 47 us -> 46 us  [body(): pl.pallas_call(render, out_shape=jax.ShapeDtypeStruct((64, LANES), jnp.fl...]
where the time goes in v5:
time: 47.6 us; the launch traced here: 47.4 us
  Pallas kernels  46 us (97%)
  local copies, waits for them, and re-layouts  1.38 us (3%)
    pallas_call x1, Pallas kernels, body(): pl.pallas_call(render, out_shape=jax.ShapeDtypeStruct((64, LANES), jnp.fl...  46 us
    unnamed x1, local copies, waits for them, and re-layouts  1.38 us

profile of v5, /device:TPU:1, one launch (start us, length us, event | category | flops | bytes accessed | tf_op | source)
XLA Modules:
  0.0 47.4 jit_solution(13129698253504569596)
XLA Ops:
  0.0 46.0 %render.1 = f32[64,128]{1,0:T(8,128)} custom-call(s32[16]{0:T(128)} %bitcast.6, s32[16]{0:T(128)} %bitcast.7, s32[16]{0:T(128)} %flips.1, f32[8]{0:T(128)} %centers_ref.1, f32[4,8]{1,0:T(4,128)} %amps_ref.1, bf16[64,32768]{1,0:T(8,128)(2,1)} %bitcast.4), custom_call_target="tpu_custom_call" | custom-call | tf_op jit(solution)/shard_map/render/pallas_call | solution.py:327
  46.0 1.4 %copy.8 = f32[4,16,128]{2,1,0:T(8,128)} copy(f32[4,16,128]{2,1,0:T(8,128)} %bitcast.5) | data formatting | bytes 65536

commit v6 on v5

--- a/solution.py
+++ b/solution.py
@@ -84,14 +84,15 @@
     return carry
 
 
-def march(vox, img, mix, even, odd, slopes, sign, quarter, group):
+def march(vox, img, mix, even, odd, slopes, sign, quarter, group, last):
     step_sign = sign * STEP
     base = (quarter * GROUPS + group) * SPANS
 
     def body(i, carry):
         set_fields(vox, mix, odd, slopes, base + 2 * i + 1)
         carry = advance(even, step_sign, carry)
-        set_fields(vox, mix, even, slopes, base + 2 * i + 2)
+        if not last:
+            set_fields(vox, mix, even, slopes, base + 2 * i + 2)
         return advance(odd, step_sign, carry)
 
     zero = jnp.zeros((N_TILE, WIDE), jnp.float32)
@@ -128,7 +129,16 @@
         part = pl.ds(pl.multiple_of(m * N_TILE, N_TILE), N_TILE)
         return pltpu.make_async_copy(blocks.at[part, :], vox.at[part, :], load_sem.at[m])
 
-    for m in range(GROUPS):
+    def first(part):
+        cells = pl.ds(part * SPAN * PIXELS, SPAN * PIXELS)
+        rows_in = pl.ds(0, N_TILE)
+        return pltpu.make_async_copy(
+            blocks.at[rows_in, cells], vox.at[rows_in, cells], load_sem.at[part * GROUPS]
+        )
+
+    for part in range(2):
+        first(part).start()
+    for m in range(1, GROUPS):
         load(m).start()
     barrier = pltpu.get_barrier_semaphore()
     for o in range(1, N_TILE):
@@ -243,18 +253,19 @@
         def _():
             share(q, my_depth // 2).wait_send()
 
-    load(0).wait()
+    first(0).wait()
     set_fields(vox, mix, even, slopes, 0)
+    first(1).wait()
     for q in range(QUARTERS):
 
-        def group(m, carry):
+        def group(m, carry, last=False):
             if q == 0:
 
                 @pl.when(m + 1 < GROUPS)
                 def _():
                     load(m + 1).wait()
 
-            march(vox, img, mix, even, odd, slopes, sign, q, m)
+            march(vox, img, mix, even, odd, slopes, sign, q, m, last)
             for o in range(N_TILE):
                 image = img[pl.ds(rows[o], 8, stride=N_TILE), :]
                 if o == 0:
@@ -266,7 +277,11 @@
                     piece(m, o).start()
             return carry
 
-        lax.fori_loop(0, GROUPS, group, 0)
+        if q < QUARTERS - 1:
+            lax.fori_loop(0, GROUPS, group, 0)
+        else:
+            lax.fori_loop(0, GROUPS - 1, group, 0)
+            group(GROUPS - 1, 0, SPANS == 2)
         if q == 0:
             pl.semaphore_wait(barrier, N_TILE + N_DEPTH - 2)
         if q < QUARTERS - 1:
@@ -345,7 +360,7 @@
             pltpu.SMEM((N_TILE,), jnp.int32),
             pltpu.SMEM((N_TILE,), jnp.int32),
             pltpu.SMEM((2 * N_TILE,), jnp.int32),
-            pltpu.SemaphoreType.DMA((GROUPS,)),
+            pltpu.SemaphoreType.DMA((GROUPS + 1,)),
             pltpu.SemaphoreType.DMA((QUARTERS - 1 + GROUPS, N_TILE)),
             pltpu.SemaphoreType.DMA((QUARTERS - 1 + GROUPS, N_TILE)),
             pltpu.SemaphoreType.DMA((QUARTERS, 4)),

time: 47.6 us -> 47 us (0.987)
  Pallas kernels: 46 us -> 45.5 us
    pallas_call x1, Pallas kernels: 46 us -> 45.5 us  [body(): pl.pallas_call(render, out_shape=jax.ShapeDtypeStruct((64, LANES), jnp.fl...]
where the time goes in v6:
time: 47 us; the launch traced here: 46.9 us
  Pallas kernels  45.5 us (97%)
  local copies, waits for them, and re-layouts  1.38 us (3%)
    pallas_call x1, Pallas kernels, body(): pl.pallas_call(render, out_shape=jax.ShapeDtypeStruct((64, LANES), jnp.fl...  45.5 us
    unnamed x1, local copies, waits for them, and re-layouts  1.38 us

profile of v6, /device:TPU:1, one launch (start us, length us, event | category | flops | bytes accessed | tf_op | source)
XLA Modules:
  0.0 46.9 jit_solution(3992416975512674890)
XLA Ops:
  0.0 45.5 %render.1 = f32[64,128]{1,0:T(8,128)} custom-call(s32[16]{0:T(128)} %bitcast.6, s32[16]{0:T(128)} %bitcast.7, s32[16]{0:T(128)} %flips.1, f32[8]{0:T(128)} %centers_ref.1, f32[4,8]{1,0:T(4,128)} %amps_ref.1, bf16[64,32768]{1,0:T(8,128)(2,1)} %bitcast.4), custom_call_target="tpu_custom_call" | custom-call | tf_op jit(solution)/shard_map/render/pallas_call | solution.py:342
  45.5 1.4 %copy.8 = f32[4,16,128]{2,1,0:T(8,128)} copy(f32[4,16,128]{2,1,0:T(8,128)} %bitcast.5) | data formatting | bytes 65536

commit v7 on v6

--- a/solution.py
+++ b/solution.py
@@ -109,6 +109,17 @@
             img[row : row + N_TILE, :] = values[c][:, side * LANES : (side + 1) * LANES]
 
 
+def neighbour(me, o):
+    return (me // 4 + o // 4) % 4 * 4 + (me % 4 + o % 4) % 4
+
+
+def hops(o):
+    return min(o // 4, 4 - o // 4) + min(o % 4, 4 - o % 4)
+
+
+FAR_FIRST = sorted(range(1, N_TILE), key=lambda o: -hops(o))
+
+
 def over(nearer, farther):
     clear = 1.0 - nearer
     left = jnp.broadcast_to(clear[3:4], (4, LANES))
@@ -143,7 +154,7 @@
     barrier = pltpu.get_barrier_semaphore()
     for o in range(1, N_TILE):
         pl.semaphore_signal(
-            barrier, inc=1, device_id={"tile": (me + o) % N_TILE}, device_id_type=MESH
+            barrier, inc=1, device_id={"tile": neighbour(me, o)}, device_id_type=MESH
         )
     for o in range(1, N_DEPTH):
         pl.semaphore_signal(
@@ -159,7 +170,7 @@
         my_position = jnp.where(order[i] == me, i, my_position)
         running = running + counts[i]
     for o in range(N_TILE):
-        tile = (me + o) % N_TILE
+        tile = neighbour(me, o)
         position = jnp.int32(0)
         for i in range(N_TILE):
             position = jnp.where(order[i] == tile, i, position)
@@ -194,7 +205,7 @@
             dst_ref=recv[q].at[pl.ds(me * GROUPS, GROUPS)],
             send_sem=send_sem.at[q, o],
             recv_sem=recv_sem.at[q, o],
-            device_id={"tile": (me + o) % N_TILE},
+            device_id={"tile": neighbour(me, o)},
             device_id_type=MESH,
         )
 
@@ -204,7 +215,7 @@
             dst_ref=recv[QUARTERS - 1].at[me * GROUPS + m],
             send_sem=send_sem.at[QUARTERS - 1 + m, o],
             recv_sem=recv_sem.at[QUARTERS - 1 + m, o],
-            device_id={"tile": (me + o) % N_TILE},
+            device_id={"tile": neighbour(me, o)},
             device_id_type=MESH,
         )
 
@@ -229,7 +240,7 @@
         return jnp.stack(parts, axis=0)
 
     def share_out(q):
-        for j in range(1, 4):
+        for j in (2, 1, 3):
             by = (my_depth // 2 + j) % 4
             dsend[q, by] = layers(q, by)
             share(q, by).start()
@@ -273,7 +284,7 @@
                 else:
                     send[q, o, m] = image
             if q == QUARTERS - 1:
-                for o in range(1, N_TILE):
+                for o in FAR_FIRST:
                     piece(m, o).start()
             return carry
 
@@ -285,7 +296,7 @@
         if q == 0:
             pl.semaphore_wait(barrier, N_TILE + N_DEPTH - 2)
         if q < QUARTERS - 1:
-            for o in range(1, N_TILE):
+            for o in FAR_FIRST:
                 exchange(q, o).start()
         if q > 0:
             for o in range(1, N_TILE):

time: 47 us -> 46.8 us (level)
  no operation moved by 1% of the time
where the time goes in v7:
time: 46.8 us; the launch traced here: 46.6 us
  Pallas kernels  45.2 us (97%)
  local copies, waits for them, and re-layouts  1.38 us (3%)
    pallas_call x1, Pallas kernels, body(): pl.pallas_call(render, out_shape=jax.ShapeDtypeStruct((64, LANES), jnp.fl...  45.2 us
    unnamed x1, local copies, waits for them, and re-layouts  1.38 us

profile of v7, /device:TPU:1, one launch (start us, length us, event | category | flops | bytes accessed | tf_op | source)
XLA Modules:
  0.0 46.6 jit_solution(10626753464770777074)
XLA Ops:
  0.0 45.2 %render.1 = f32[64,128]{1,0:T(8,128)} custom-call(s32[16]{0:T(128)} %bitcast.6, s32[16]{0:T(128)} %bitcast.7, s32[16]{0:T(128)} %flips.1, f32[8]{0:T(128)} %centers_ref.1, f32[4,8]{1,0:T(4,128)} %amps_ref.1, bf16[64,32768]{1,0:T(8,128)(2,1)} %bitcast.4), custom_call_target="tpu_custom_call" | custom-call | tf_op jit(solution)/shard_map/render/pallas_call | solution.py:353
  45.2 1.4 %copy.8 = f32[4,16,128]{2,1,0:T(8,128)} copy(f32[4,16,128]{2,1,0:T(8,128)} %bitcast.5) | data formatting | bytes 65536
